TPU v7x, 32 devices: a whole 2x2x4 slice. The times are simulated.
32 devices in a mesh: seq: 4 (over z), head: 8 (over y, x, core).
Axes of the slice: x: 2, y: 2, z: 4, core: 2. Of those that a mesh axis runs over, the one named last changes fastest.
Arguments:
- queries: bfloat16 [4096, 2048], P(('seq', 'head')), may hold values from -6 to 6
- key_rows: bfloat16 [4096, 2048], P(('seq', 'head')), may hold values from -6 to 6
- value_rows: bfloat16 [4096, 2048], P(('seq', 'head')), may hold values from -6 to 6
- ridge_diag: float32 [16, 128], replicated, may hold values from 0.5 to 4
Outputs:
- mixed: bfloat16 [4096, 2048], P(('seq', 'head'))
All inputs are finite; a program needn't handle non-finite values.
Results may differ from a plain program's by a relative error of at most 0.0075.
The roundings to bfloat16 on the way count: a program that leaves them out, or rounds other values in their place, can miss the bound.
Values may be sent and summed in bfloat16 or wider, within the bound.
A program may use at most 64 MiB of HBM per device.

v0:
```python
import jax
import jax.numpy as jnp
from jax import lax
from jax.sharding import PartitionSpec as P

DK = 128
GROUP = 64


epsilon = 1e-06
highest = lax.Precision.HIGHEST


def prefix_2(value, axis, join, neutral):
    count, mine = (lax.axis_size(axis), lax.axis_index(axis))
    pieces = jax.tree.map(lambda part: lax.all_gather(part, axis), value)
    running = jax.tree.map(
        lambda part, zero: jnp.full_like(part, 0) + jnp.asarray(zero, part.dtype), value, neutral
    )

    def turn(position, running):
        longer = join(running, jax.tree.map(lambda part: part[position], pieces))
        return jax.tree.map(lambda new, old: jnp.where(position < mine, new, old), longer, running)

    return lax.fori_loop(0, count - 1, turn, running)


def unit_rows(matrix):
    values_f = matrix.astype(jnp.float32)
    scale_back = lax.rsqrt(jnp.sum(values_f * values_f, axis=-1, keepdims=True) + epsilon)
    return (values_f * scale_back).astype(jnp.bfloat16)


def add_pair(earlier, later):
    return (earlier[0] + later[0], earlier[1] + later[1])


def times_plain(left, right):
    return jnp.einsum("...ij,...jk->...ik", left, right, precision=highest)


def times_turned(left, right):
    return jnp.einsum("...ij,...kj->...ik", left, right, precision=highest)


def turned_times(left, right):
    return jnp.einsum("...ji,...jk->...ik", left, right, precision=highest)


def factor_solve(system, targets):
    width = system.shape[-1]
    edge = min(32, width)
    count = width // edge

    def part(i, j):
        return system[..., i * edge : (i + 1) * edge, j * edge : (j + 1) * edge]

    lower = {}
    inverses = []
    for j in range(count):
        pivot = part(j, j)
        for k in range(j):
            pivot = pivot - times_turned(lower[j, k], lower[j, k])
        pivot_factor = jnp.linalg.cholesky(pivot)
        identity = jnp.broadcast_to(jnp.eye(edge, dtype=jnp.float32), pivot_factor.shape)
        inverse = jax.scipy.linalg.solve_triangular(pivot_factor, identity, lower=True)
        inverses.append(inverse)
        for i in range(j + 1, count):
            below = part(i, j)
            for k in range(j):
                below = below - times_turned(lower[i, k], lower[j, k])
            lower[i, j] = times_turned(below, inverse)
    forward = []
    for j in range(count):
        rest = targets[..., j * edge : (j + 1) * edge, :]
        for k in range(j):
            rest = rest - times_plain(lower[j, k], forward[k])
        forward.append(times_plain(inverses[j], rest))
    backward = [None] * count
    for j in reversed(range(count)):
        rest = forward[j]
        for k in range(j + 1, count):
            rest = rest - turned_times(lower[k, j], backward[k])
        backward[j] = turned_times(inverses[j], rest)
    return jnp.concatenate(backward, axis=-2)


def mesa_block(queries, key_rows, value_rows, ridge_here, prefix):
    row_count = queries.shape[0]
    heads_here = queries.shape[1] // DK
    groups = row_count // GROUP

    def by_group(matrix):
        return jnp.transpose(matrix.reshape(groups, GROUP, heads_here, DK), (2, 0, 1, 3))

    q_unit = by_group(unit_rows(queries.reshape(row_count, heads_here, DK)))
    k_unit = by_group(unit_rows(key_rows.reshape(row_count, heads_here, DK)))
    v_block = by_group(value_rows)
    group_gram = jnp.einsum("hcti,hctj->hcij", k_unit, k_unit, preferred_element_type=jnp.float32)
    group_vk = jnp.einsum("hctv,hctk->hcvk", v_block, k_unit, preferred_element_type=jnp.float32)
    gram_inc = jnp.cumsum(group_gram, axis=1)
    vk_inc = jnp.cumsum(group_vk, axis=1)
    gram_pre, vk_pre = prefix((gram_inc[:, -1], vk_inc[:, -1]))
    gram_start = gram_pre[:, None] + gram_inc - group_gram
    vk_start = vk_pre[:, None] + vk_inc - group_vk
    system = gram_start + ridge_here[:, None, :, None] * jnp.eye(DK, dtype=jnp.float32)
    targets = jnp.swapaxes(q_unit.astype(jnp.float32), -1, -2)
    solved = factor_solve(system, targets)
    k_f = k_unit.astype(jnp.float32)
    carried = jnp.einsum("hcvk,hckt->hctv", vk_start, solved, precision=highest)
    scores = jnp.einsum("hcsk,hckt->hcts", k_f, solved, precision=highest)
    causal = jnp.arange(GROUP)[None, :] <= jnp.arange(GROUP)[:, None]
    within = jnp.einsum(
        "hcts,hcsv->hctv",
        jnp.where(causal, scores, 0.0),
        v_block.astype(jnp.float32),
        precision=highest,
    )
    result = (carried + within).astype(jnp.bfloat16)
    return jnp.transpose(result, (1, 2, 0, 3)).reshape(row_count, heads_here * DK)


def body(queries, key_rows, value_rows, ridge_diag):

    def state_moves(totals):
        outward = (
            lax.all_to_all(totals[0][None], "head", split_axis=1, concat_axis=0, tiled=True),
            lax.all_to_all(totals[1][None], "head", split_axis=1, concat_axis=0, tiled=True),
        )
        gram_inc = jnp.cumsum(outward[0], axis=0)
        vk_inc = jnp.cumsum(outward[1], axis=0)
        gram_before = gram_inc - outward[0]
        vk_before = vk_inc - outward[1]
        shard_totals = (gram_inc[-1], vk_inc[-1])
        empty = (jnp.zeros_like(shard_totals[0]), jnp.zeros_like(shard_totals[1]))
        seq_pre = prefix_2(shard_totals, "seq", add_pair, empty)
        starts = (seq_pre[0][None] + gram_before, seq_pre[1][None] + vk_before)
        returned = (
            lax.all_to_all(starts[0], "head", split_axis=0, concat_axis=1, tiled=True),
            lax.all_to_all(starts[1], "head", split_axis=0, concat_axis=1, tiled=True),
        )
        return (returned[0][0], returned[1][0])

    return mesa_block(queries, key_rows, value_rows, ridge_diag, state_moves)


def solution(mesh):
    in_specs = (P(("seq", "head"), None), P(("seq", "head"), None), P(("seq", "head"), None), P())
    out_specs = P(("seq", "head"), None)
    return jax.shard_map(body, mesh=mesh, in_specs=in_specs, out_specs=out_specs, check_vma=False)
```

profile of v0, /device:TPU:0, one launch (start us, length us, event | category | flops | bytes accessed | tf_op | source)
XLA Modules:
  0.0 884.7 jit_solution(14811109984627336001)
XLA Ops:
  7.9 5.2 all-to-all-start
  22.5 5.9 all-to-all-done
  28.4 3.6 all-to-all-start.1
  34.7 16.8 %all_gather.6 = f32[4,2,128,128]{3,2,1,0:T(8,128)} all-gather(f32[1,2,128,128]{3,2,1,0:T(8,128)S(1)} %slice.81), channel_id=1, replica_groups=mesh['seq'=4,'head'=8] {'seq'}, dimensions={0}, use_global_device_ids=true | all-gather | bytes 655360 | tf_op jit(solution)/shard_map/all_gather | solution.py:16
  56.1 16.6 %all_gather.7 = f32[4,2,128,128]{3,2,1,0:T(8,128)} all-gather(f32[1,2,128,128]{3,2,1,0:T(8,128)S(1)} %slice.83), channel_id=1, replica_groups=mesh['seq'=4,'head'=8] {'seq'}, dimensions={0}, use_global_device_ids=true | all-gather | bytes 655360 | tf_op jit(solution)/shard_map/all_gather | solution.py:16
  72.7 3.2 while.16
  77.0 4.4 all-to-all-start.2
  88.9 8.0 all-to-all-done.2
  96.9 4.2 all-to-all-start.3
  101.2 2.6 copy.198
  103.7 3.1 subtract_add_fusion
  107.2 93.8 %custom-call.14 = f32[16,2,32,32]{3,2,1,0:T(8,128)S(1)} custom-call(f32[16,2,32,32]{3,2,1,0:T(8,128)S(1)} %fusion.30), custom_call_target="Cholesky" | custom-call | tf_op jit(solution)/shard_map/jit(cholesky)/cholesky | solution.py:64
  201.6 79.3 %custom-call.15 = f32[16,2,1,32,32]{3,4,2,1,0:T(8,128)S(1)} custom-call(f32[16,2,1,32,32]{4,3,2,1,0:T(8,128)S(1)} %select_bitcast_fusion.3), custom_call_target="InvertDiagBlocksLowerTriangular" | custom-call | tf_op jit(solution)/shard_map/jit(_solve_triangular)/vmap(vmap())/triangular_solve | solution.py:66
  302.5 93.8 %custom-call.16 = f32[16,2,32,32]{3,2,1,0:T(8,128)S(1)} custom-call(f32[16,2,32,32]{3,2,1,0:T(8,128)S(1)} %fusion.27), custom_call_target="Cholesky" | custom-call | tf_op jit(solution)/shard_map/jit(cholesky)/cholesky | solution.py:64
  396.9 79.5 %custom-call.17 = f32[16,2,1,32,32]{3,4,2,1,0:T(8,128)} custom-call(f32[16,2,1,32,32]{4,3,2,1,0:T(8,128)S(1)} %select_bitcast_fusion.2), custom_call_target="InvertDiagBlocksLowerTriangular" | custom-call | tf_op jit(solution)/shard_map/jit(_solve_triangular)/vmap(vmap())/triangular_solve | solution.py:66
  476.4 2.1 fusion.25
  488.0 94.4 %custom-call.18 = f32[16,2,32,32]{3,2,1,0:T(8,128)S(1)} custom-call(f32[16,2,32,32]{3,2,1,0:T(8,128)} %fusion.24), custom_call_target="Cholesky" | custom-call | tf_op jit(solution)/shard_map/jit(cholesky)/cholesky | solution.py:64
  583.8 79.5 %custom-call.19 = f32[16,2,1,32,32]{3,4,2,1,0:T(8,128)S(1)} custom-call(f32[16,2,1,32,32]{4,3,2,1,0:T(8,128)} %select_bitcast_fusion.1), custom_call_target="InvertDiagBlocksLowerTriangular" | custom-call | tf_op jit(solution)/shard_map/jit(_solve_triangular)/vmap(vmap())/triangular_solve | solution.py:66
  671.1 2.1 fusion.21
  673.2 95.1 %custom-call.20 = f32[16,2,32,32]{3,2,1,0:T(8,128)} custom-call(f32[16,2,32,32]{3,2,1,0:T(8,128)} %fusion.21), custom_call_target="Cholesky" | custom-call | tf_op jit(solution)/shard_map/jit(cholesky)/cholesky | solution.py:64
  771.7 80.4 %custom-call.21 = f32[16,2,1,32,32]{3,4,2,1,0:T(8,128)} custom-call(f32[16,2,1,32,32]{4,3,2,1,0:T(8,128)} %select_bitcast_fusion), custom_call_target="InvertDiagBlocksLowerTriangular" | custom-call | tf_op jit(solution)/shard_map/jit(_solve_triangular)/vmap(vmap())/triangular_solve | solution.py:66
  852.1 2.1 fusion.19
  874.2 2.6 copy.245
  876.8 6.1 fusion.6
  (193 shorter events, 102.3 us)
Async XLA Ops:
  3.6 14.7 %copy-start.15 = (bf16[16,2,64,128]{3,2,1,0:T(8,128)(2,1)}, bf16[16,2,64,128]{3,2,1,0:T(8,128)(2,1)S(1)}, u32[]{:S(2)}) copy-start(bf16[16,2,64,128]{3,2,1,0:T(8,128)(2,1)S(1)} %fusion.12) | copy-start | bytes 1572868
  6.7 7.0 copy-start.29
  7.9 20.6 %all-to-all-start = ((f32[1,16,128,128]{2,3,0,1:T(8,128)}), f32[1,16,128,128]{2,3,0,1:T(8,128)S(1)}, u32[]{:S(2)}, u32[]{:S(2)}) async-start(f32[1,16,128,128]{2,3,0,1:T(8,128)} %slice_bitcast_fusion.1), calls=%async_computation | async-start | bytes 2097152 | tf_op jit(solution)/shard_map/all_to_all | solution.py:127
  15.6 3.3 copy-start.23
  21.5 10.6 %copy-start.30 = (bf16[128,2048]{1,0:T(8,128)(2,1)S(1)}, bf16[128,2048]{1,0:T(8,128)(2,1)}, u32[]{:S(2)}) copy-start(bf16[128,2048]{1,0:T(8,128)(2,1)} %param.9) | copy-start | bytes 1572868
  28.4 23.0 %all-to-all-start.1 = ((f32[1,16,128,128]{2,3,0,1:T(8,128)}), f32[1,16,128,128]{2,3,0,1:T(8,128)S(1)}, u32[]{:S(2)}, u32[]{:S(2)}) async-start(f32[1,16,128,128]{2,3,0,1:T(8,128)} %slice_bitcast_fusion), calls=%async_computation.1 | async-start | bytes 2097152 | tf_op jit(solution)/shard_map/all_to_all | solution.py:128
  77.0 4.4 copy-start.26
  77.0 19.9 %all-to-all-start.2 = ((f32[8,2,128,128]{3,2,1,0:T(8,128)}), f32[8,2,128,128]{3,2,1,0:T(8,128)}, u32[]{:S(2)}, u32[]{:S(2)}) async-start(f32[8,2,128,128]{3,2,1,0:T(8,128)} %subtract_add_fusion.2), calls=%async_computation.2 | async-start | bytes 2097152 | tf_op jit(solution)/shard_map/all_to_all | solution.py:139
  88.9 14.8 %copy-start.28 = (f32[16,128,128]{1,2,0:T(8,128)S(1)}, f32[16,128,128]{1,2,0:T(8,128)}, u32[]{:S(2)}) copy-start(f32[16,128,128]{1,2,0:T(8,128)} %broadcast_multiply_fusion) | copy-start | bytes 3145732
  96.9 777.3 %all-to-all-start.3 = ((f32[8,2,128,128]{3,2,1,0:T(8,128)}), f32[8,2,128,128]{3,2,1,0:T(8,128)}, u32[]{:S(2)}, u32[]{:S(2)}) async-start(f32[8,2,128,128]{3,2,1,0:T(8,128)} %subtract_add_fusion.1), calls=%async_computation.3 | async-start | bytes 2097152 | tf_op jit(solution)/shard_map/all_to_all | solution.py:140
  106.8 94.6 %copy-start.40 = (pred[32,32]{1,0:T(8,128)(4,1)S(1)}, pred[32,32]{1,0:T(8,128)(4,1)}, u32[]{:S(2)}) copy-start(pred[32,32]{1,0:T(8,128)(4,1)} %iota_compare_fusion.2) | copy-start | bytes 3076
  281.8 14.4 %copy-start.2 = (f32[16,2,32,32]{3,2,1,0:T(8,128)}, f32[16,2,32,32]{3,2,1,0:T(8,128)S(1)}, u32[]{:S(2)}) copy-start(f32[16,2,32,32]{3,2,1,0:T(8,128)S(1)} %fusion.28) | copy-start | bytes 393220
  290.9 9.6 %copy-start = (f32[16,2,32,32]{3,2,1,0:T(8,128)}, f32[16,2,32,32]{3,2,1,0:T(8,128)S(1)}, u32[]{:S(2)}) copy-start(f32[16,2,32,32]{3,2,1,0:T(8,128)S(1)} %fusion.15) | copy-start | bytes 393220
  302.4 176.1 %copy-start.32 = (f32[16,2,32,32]{2,3,1,0:T(8,128)S(1)}, f32[16,2,32,32]{2,3,1,0:T(8,128)}, u32[]{:S(2)}) copy-start(f32[16,2,32,32]{2,3,1,0:T(8,128)} %convolution_subtract_fusion.13) | copy-start | bytes 393220
  396.2 83.3 %copy-start.33 = (f32[16,2,32,32]{2,3,1,0:T(8,128)S(1)}, f32[16,2,32,32]{2,3,1,0:T(8,128)}, u32[]{:S(2)}) copy-start(f32[16,2,32,32]{2,3,1,0:T(8,128)} %convolution_subtract_fusion.19) | copy-start | bytes 393220
  476.4 4.2 copy-start.36
  480.6 3.5 copy-start.38
  663.3 3.9 copy-start.39
  667.3 190.7 %copy-start.8 = (f32[16,2,32,32]{3,2,1,0:T(8,128)}, f32[16,2,32,32]{3,2,1,0:T(8,128)S(1)}, u32[]{:S(2)}) copy-start(f32[16,2,32,32]{3,2,1,0:T(8,128)S(1)} %fusion.57) | copy-start | bytes 393220
  852.1 3.9 copy-start.34
  862.3 7.5 copy-start.17
  865.4 4.4 copy-start.22
  872.5 4.2 copy-start.5
  872.5 4.2 copy-start.18
  (23 other events, 44.2 us)
where the time goes:
time: 892 us; the launch traced here: 885 us
  other arithmetic  729 us (82%)
  matrix products  62.6 us (7%)
  blocking collectives  33.4 us (4%)
  local copies, waits for them, and re-layouts  27 us (3%)
  starting transfers between devices  17.4 us (2%)
  waiting for transfers between devices  13.9 us (2%)
    another operation x13, other arithmetic, factor_solve(): pivot_factor = jnp.linalg.cholesky(pivot)  380 us
    another operation x9, other arithmetic, factor_solve(): jax.scipy.linalg.solve_triangular(pivot_factor, identity, lower=True)  322 us
    all_gather x2, blocking collectives, prefix_2(): pieces = jax.tree.map(lambda part: lax.all_gather(part, axis), value)  33.4 us
    dot_general x16, matrix products, times_turned(): return jnp.einsum('...ij,...kj->...ik', left, right, precision=highest)  24.7 us
  transfers between devices with their start and end apart: 4, of which 2 were waited for; matrix products, arithmetic and copies ran while one was open for 89% of the time, Pallas kernels for 0%

commit v1 on v0

v1 whole, which is shorter than its diff:
```python
import functools

import jax
import jax.numpy as jnp
from jax import lax
from jax.experimental import pallas as pl
from jax.experimental.pallas import tpu as pltpu
from jax.sharding import PartitionSpec as P

DK = 128
GROUP = 64
EDGE = 32
PACK = DK // EDGE
EPS = 1e-06
F32 = jnp.float32
BF16 = jnp.bfloat16


def unit(rows):
    wide = rows.astype(F32)
    back = lax.rsqrt(jnp.sum(wide * wide, axis=-1, keepdims=True) + EPS)
    return (wide * back).astype(BF16)


def split3(value):
    high = value.astype(BF16)
    rest = value - high.astype(F32)
    mid = rest.astype(BF16)
    low = (rest - mid.astype(F32)).astype(BF16)
    return high, mid, low


def dot(left, right, contract):
    return lax.dot_general(left, right, ((contract[:1], contract[1:]), ((), ())), preferred_element_type=F32)


def left_stack(parts):
    high, mid, low = parts
    return jnp.concatenate([high, high, mid, high, low, mid], axis=0)


def right_stack(parts):
    high, mid, low = parts
    return jnp.concatenate([high, mid, high, low, high, mid], axis=0)


def sweep_pack(rows, lane, sub):
    base = (lane // EDGE) * EDGE
    within = lane - base
    for j in range(EDGE):
        at, inner = j // 8, j % 8
        column = within == j
        pick = base + j
        pivot_row = jnp.broadcast_to(rows[at][inner : inner + 1, :], rows[at].shape)
        pivot = jnp.take_along_axis(pivot_row, pick, axis=1, mode="promise_in_bounds")
        scaled = jnp.where(column, -1.0, pivot_row) * (1.0 / pivot)
        fresh = []
        for v, block in enumerate(rows):
            col = jnp.take_along_axis(block, pick, axis=1, mode="promise_in_bounds")
            gone = column
            if v == at:
                here = sub == inner
                col = jnp.where(here, -1.0, col)
                gone = jnp.logical_or(column, here)
            fresh.append(jnp.where(gone, 0.0, block) - col * scaled)
        rows = fresh
    return rows


def totals_kernel(k_ref, v_ref, ku_ref, tot_ref):
    heads = k_ref.shape[1] // DK
    for h in range(heads):
        cols = slice(h * DK, (h + 1) * DK)
        ku = unit(k_ref[:, cols])
        ku_ref[:, cols] = ku
        both = jnp.concatenate([ku, v_ref[:, cols]], axis=1)
        tot_ref[h] = dot(ku, both, (0, 0))


def invert_all(sys_ref, pinv_ref):
    count = sys_ref.shape[0]
    packs = count // PACK
    lane = lax.broadcasted_iota(jnp.int32, (8, DK), 1)
    sub = lax.broadcasted_iota(jnp.int32, (8, DK), 0)
    lane32 = lax.broadcasted_iota(jnp.int32, (EDGE, DK), 1)
    sub32 = lax.broadcasted_iota(jnp.int32, (EDGE, DK), 0)
    row128 = lax.broadcasted_iota(jnp.int32, (DK, DK), 0) // EDGE
    lane128 = lax.broadcasted_iota(jnp.int32, (DK, DK), 1) // EDGE

    def panel(p, carry):
        start = pl.multiple_of(p * EDGE, EDGE)
        all_rows = []
        for g in range(packs):
            packed = None
            for k in range(PACK):
                piece = sys_ref[g * PACK + k, pl.ds(start, EDGE), :]
                piece = pltpu.roll(piece, lax.rem((k - p) * EDGE + DK, DK), 1)
                packed = piece if packed is None else jnp.where(lane32 // EDGE == k, piece, packed)
            all_rows.append([packed[8 * v : 8 * v + 8, :] for v in range(EDGE // 8)])
        for g in range(packs):
            done = sweep_pack(all_rows[g], lane, sub)
            pinv_ref[g] = jnp.concatenate(done, axis=0)

        mine = lane32 // EDGE == p
        diag = lane32 - p * EDGE == sub32
        cleared = jnp.logical_or(row128 == p, lane128 == p)

        def update(g, carry):
            inverse = left_stack(split3(pinv_ref[g]))
            for k in range(PACK):
                s = g * PACK + k
                rows = sys_ref[s, pl.ds(start, EDGE), :]
                rows = jnp.where(mine, jnp.where(diag, -1.0, 0.0), rows)
                parts = split3(rows)
                full = dot(inverse, right_stack(parts), (0, 0))
                scaled = full[k * EDGE : (k + 1) * EDGE, :]
                change = dot(left_stack(parts), right_stack(split3(scaled)), (0, 0))
                sys_ref[s] = jnp.where(cleared, 0.0, sys_ref[s]) + change
            return carry

        return lax.fori_loop(0, packs, update, carry)

    lax.fori_loop(0, PACK, panel, 0)


def build_systems(ku_ref, v_ref, pre_ref, ridge_ref, sys_ref, vk_ref):
    groups = ku_ref.shape[0] // GROUP
    heads = ku_ref.shape[1] // DK
    eye = lax.broadcasted_iota(jnp.int32, (DK, DK), 0) == lax.broadcasted_iota(jnp.int32, (DK, DK), 1)
    for h in range(heads):
        cols = slice(h * DK, (h + 1) * DK)
        ridge = jnp.where(eye, ridge_ref[h : h + 1, :], 0.0)

        def step(c, run):
            rows = pl.ds(pl.multiple_of(c * GROUP, GROUP), GROUP)
            sys_ref[h * groups + c] = run[:, :DK] + ridge
            vk_ref[h * groups + c] = run[:, DK:]
            ku = ku_ref[rows, cols]
            return run + dot(ku, jnp.concatenate([ku, v_ref[rows, cols]], axis=1), (0, 0))

        lax.fori_loop(0, groups, step, pre_ref[h])


def finish(q_ref, ku_ref, v_ref, sys_ref, vk_ref, out_ref):
    groups = ku_ref.shape[0] // GROUP
    heads = ku_ref.shape[1] // DK
    causal = lax.broadcasted_iota(jnp.int32, (GROUP, GROUP), 1) <= lax.broadcasted_iota(jnp.int32, (GROUP, GROUP), 0)
    for h in range(heads):
        cols = slice(h * DK, (h + 1) * DK)

        def step(c, carry):
            rows = pl.ds(pl.multiple_of(c * GROUP, GROUP), GROUP)
            qu = unit(q_ref[rows, cols])
            high, mid, low = split3(sys_ref[h * groups + c])
            solved = -(dot(qu, high, (1, 0)) + (dot(qu, mid, (1, 0)) + dot(qu, low, (1, 0))))
            shigh, smid, slow = split3(solved)
            vhigh, vmid, vlow = split3(vk_ref[h * groups + c])
            carried = dot(shigh, vhigh, (1, 0)) + (
                dot(shigh, vmid, (1, 0)) + dot(smid, vhigh, (1, 0)) + (
                    dot(smid, vmid, (1, 0)) + dot(shigh, vlow, (1, 0)) + dot(slow, vhigh, (1, 0))))
            ku = ku_ref[rows, cols]
            scores = dot(shigh, ku, (1, 1)) + (dot(smid, ku, (1, 1)) + dot(slow, ku, (1, 1)))
            chigh, cmid, clow = split3(jnp.where(causal, scores, 0.0))
            vb = v_ref[rows, cols]
            inner = dot(chigh, vb, (1, 0)) + (dot(cmid, vb, (1, 0)) + dot(clow, vb, (1, 0)))
            out_ref[rows, cols] = (carried + inner).astype(BF16)
            return carry

        lax.fori_loop(0, groups, step, 0)


def solve_kernel(q_ref, ku_ref, v_ref, pre_ref, ridge_ref, out_ref, sys_ref, vk_ref, pinv_ref):
    build_systems(ku_ref, v_ref, pre_ref, ridge_ref, sys_ref, vk_ref)
    invert_all(sys_ref, pinv_ref)
    finish(q_ref, ku_ref, v_ref, sys_ref, vk_ref, out_ref)


def body(queries, key_rows, value_rows, ridge_diag):
    owners = lax.axis_size("head")
    heads = queries.shape[1] // DK // owners
    width = heads * DK

    def spread(rows):
        return lax.all_to_all(rows, "head", split_axis=1, concat_axis=0, tiled=True)

    k_all, v_all, q_all = spread(key_rows), spread(value_rows), spread(queries)
    tokens = k_all.shape[0]
    systems = heads * (tokens // GROUP)
    vmem = pl.BlockSpec(memory_space=pltpu.VMEM)
    ku, total = pl.pallas_call(
        totals_kernel,
        out_shape=(
            jax.ShapeDtypeStruct((tokens, width), BF16),
            jax.ShapeDtypeStruct((heads, DK, 2 * DK), F32),
        ),
        in_specs=[vmem] * 2,
        out_specs=(vmem, vmem),
    )(k_all, v_all)
    gathered = lax.all_gather(total, "seq")
    mine = lax.axis_index("seq")
    before = jnp.arange(lax.axis_size("seq")) < mine
    pre = jnp.sum(jnp.where(before[:, None, None, None], gathered, 0.0), axis=0)
    ridge = lax.dynamic_slice_in_dim(ridge_diag, lax.axis_index("head") * heads, heads, 0)
    out = pl.pallas_call(
        solve_kernel,
        out_shape=jax.ShapeDtypeStruct((tokens, width), BF16),
        in_specs=[vmem] * 5,
        out_specs=vmem,
        scratch_shapes=[
            pltpu.VMEM((systems, DK, DK), F32),
            pltpu.VMEM((systems, DK, DK), F32),
            pltpu.VMEM((systems // PACK, EDGE, DK), F32),
        ],
        compiler_params=pltpu.CompilerParams(vmem_limit_bytes=48 * 1024 * 1024),
    )(q_all, ku, v_all, pre, ridge)
    return lax.all_to_all(out, "head", split_axis=0, concat_axis=1, tiled=True)


def solution(mesh):
    in_specs = (P(("seq", "head"), None), P(("seq", "head"), None), P(("seq", "head"), None), P())
    out_specs = P(("seq", "head"), None)
    return jax.shard_map(body, mesh=mesh, in_specs=in_specs, out_specs=out_specs, check_vma=False)
```

time: 892 us -> 174 us (0.20)
  other arithmetic: 729 us -> 1.48 us
  Pallas kernels: 0 us -> 87.8 us
  matrix products: 62.6 us -> 0 us
  local copies, waits for them, and re-layouts: 27 us -> 3.64 us
  waiting for transfers between devices: 13.9 us -> 32.7 us
  between operations: 1.33 us -> 13.5 us
    another operation x26 -> x0, other arithmetic: 707 us -> none  [the longest x13 380 us: factor_solve(): pivot_factor = jnp.linalg.cholesky(pivot)]
    pallas_call x0 -> x2, Pallas kernels: none -> 87.8 us  [the longest x1 85.2 us: body(): pl.pallas_call(solve_kernel, out_shape=jax.ShapeDtypeStruct((tokens, widt...]
    dot_general x41 -> x0, matrix products: 56.4 us -> none  [the longest x16 24.7 us: times_turned(): return jnp.einsum('...ij,...kj->...ik', left, right, precision=highest)]
    all_gather x2 -> x0, blocking collectives: 33.4 us -> none  [prefix_2(): pieces = jax.tree.map(lambda part: lax.all_gather(part, axis), value)]
    all_to_all x0 -> x2, blocking collectives: none -> 26 us  [the longest x1 13.2 us: body(): return lax.all_to_all(out, 'head', split_axis=0, concat_axis=1, tiled=True)]
    all_gather x0 -> x1, waiting for transfers between devices: none -> 23.1 us  [body(): gathered = lax.all_gather(total, 'seq')]
    unnamed x92 -> x12, local copies, waits for them, and re-layouts: 11.8 us -> 0.03 us
  transfers between devices with their start and end apart: 4 -> 3, of which waited for: 2 -> 2; matrix products, arithmetic and copies ran while one was open for 89% -> 1% of each run, Pallas kernels for 0% -> 0%
where the time goes in v1:
time: 174 us
  Pallas kernels  87.8 us (50%)
  waiting for transfers between devices  32.7 us (19%)
  blocking collectives  26 us (15%)
  between operations  13.5 us (8%)
  starting transfers between devices  8.86 us (5%)
  local copies, waits for them, and re-layouts  3.64 us (2%)
    pallas_call x1, Pallas kernels, body(): pl.pallas_call(solve_kernel, out_shape=jax.ShapeDtypeStruct((tokens, widt...  85.2 us
    all_gather x1, waiting for transfers between devices, body(): gathered = lax.all_gather(total, 'seq')  23.1 us
    all_to_all x1, blocking collectives, body(): return lax.all_to_all(out, 'head', split_axis=0, concat_axis=1, tiled=True)  13.2 us
    all_to_all x1, blocking collectives, spread(): return lax.all_to_all(rows, 'head', split_axis=1, concat_axis=0, tiled=True)  12.8 us
    all_to_all x2, waiting for transfers between devices, spread(): return lax.all_to_all(rows, 'head', split_axis=1, concat_axis=0, tiled=True)  9.62 us
    all_to_all x2, starting transfers between devices, spread(): return lax.all_to_all(rows, 'head', split_axis=1, concat_axis=0, tiled=True)  8.82 us
  transfers between devices with their start and end apart: 3, of which 2 were waited for; matrix products, arithmetic and copies ran while one was open for 1% of the time, Pallas kernels for 0%

profile of v1, /device:TPU:0, one launch (start us, length us, event | category | flops | bytes accessed | tf_op | source)
XLA Modules:
  0.0 174.0 jit_solution(6144795115569919468)
XLA Ops:
  6.5 0.0 copy-start
  6.5 1.9 %copy.20 = bf16[16,8,8,256]{3,2,0,1:T(8,128)(2,1)} copy(bf16[16,8,8,256]{3,2,1,0:T(8,128)(2,1)} %bitcast.34) | data formatting | bytes 1048576 | tf_op jit(solution)/shard_map/all_to_all | solution.py:184
  8.4 0.0 copy-start.4
  8.4 5.3 %all-to-all-start.2 = ((bf16[128,8,256]{2,0,1:T(8,128)(2,1)}), bf16[128,8,256]{2,0,1:T(8,128)(2,1)S(1)}, u32[]{:S(2)}, u32[]{:S(2)}) async-start(bf16[128,8,256]{2,0,1:T(8,128)(2,1)} %bitcast.23), calls=%async_computation.2 | async-start | bytes 1048576 | tf_op jit(solution)/shard_map/all_to_all | solution.py:184
  13.8 0.0 all-gather.3.cloned.1.call-start
  13.8 0.0 copy-done.4
  13.8 9.6 %all-to-all-done.2 = bf16[128,8,256]{2,0,1:T(8,128)(2,1)S(1)} async-done(((bf16[128,8,256]{2,0,1:T(8,128)(2,1)}), bf16[128,8,256]{2,0,1:T(8,128)(2,1)S(1)}, u32[]{:S(2)}, u32[]{:S(2)}) %all-to-all-start.2) | async-done | bytes 524320 | tf_op jit(solution)/shard_map/all_to_all | solution.py:184
  23.5 0.0 copy-start.1
  23.5 12.8 %all_to_all.76 = bf16[128,8,256]{2,0,1:T(8,128)(2,1)} all-to-all(bf16[128,8,256]{2,0,1:T(8,128)(2,1)S(1)} %bitcast.30), channel_id=1, replica_groups=mesh['seq'=4,'head'=8] {'head'}, dimensions={1} | all-to-all | bytes 1048576 | tf_op jit(solution)/shard_map/all_to_all | solution.py:184
  36.3 0.0 copy-done.1
  36.3 2.6 %shard_map.46 = (bf16[1024,256]{1,0:T(8,128)(2,1)}, f32[2,128,256]{2,1,0:T(8,128)}) custom-call(bf16[1024,256]{1,0:T(8,128)(2,1)} %bitcast.31, bf16[1024,256]{1,0:T(8,128)(2,1)} %bitcast.26), custom_call_target="tpu_custom_call" | custom-call | tf_op jit(solution)/shard_map/pallas_call | solution.py:190
  38.9 0.0 all-gather.3.cloned.1.call-update
  38.9 0.0 copy-done.5
  38.9 0.8 copy.22
  39.7 3.5 %all-to-all-start = ((bf16[128,8,256]{2,0,1:T(8,128)(2,1)}), bf16[128,8,256]{2,0,1:T(8,128)(2,1)S(1)}, u32[]{:S(2)}, u32[]{:S(2)}) async-start(bf16[128,8,256]{2,0,1:T(8,128)(2,1)} %bitcast.25), calls=%async_computation | async-start | bytes 1048576 | tf_op jit(solution)/shard_map/all_to_all | solution.py:184
  43.2 0.0 copy-done
  43.3 23.1 %all-gather.3.cloned.1.call-done = f32[8,128,256]{2,1,0:T(8,128)} async-done(((f32[2,128,256]{2,1,0:T(8,128)}), f32[8,128,256]{2,1,0:T(8,128)}) %all-gather.3.cloned.1.call-update) | async-done | bytes 1048592 | tf_op jit(solution)/shard_map/all_gather | solution.py:199
  66.4 1.5 select_reduce_fusion.pre_ref
  67.9 0.0 all-to-all-done
  67.9 0.0 copy-done.2
  67.9 0.0 copy-done.3
  67.9 85.2 %shard_map.47 = bf16[1024,256]{1,0:T(8,128)(2,1)S(1)} custom-call(bf16[1024,256]{1,0:T(8,128)(2,1)S(1)} %bitcast.28, bf16[1024,256]{1,0:T(8,128)(2,1)S(1)} %copy-done.3, bf16[1024,256]{1,0:T(8,128)(2,1)S(1)} %bitcast.27, f32[2,128,256]{2,1,0:T(8,128)S(1)} %select_reduce_fusion.pre_ref, f32[2,128]{1,0:T(2,128)S(1)} %constant_dynamic-slice_fusion.ridge_ref), custom_call_target="tpu_custom_call" | custom-call | tf_op jit(solution)/shard_map/pallas_call | solution.py:204
  153.1 13.2 %all_to_all.77 = bf16[8,128,256]{2,1,0:T(8,128)(2,1)S(1)} all-to-all(bf16[8,128,256]{2,1,0:T(8,128)(2,1)S(1)} %bitcast.29), channel_id=1, replica_groups=mesh['seq'=4,'head'=8] {'head'}, dimensions={0} | all-to-all | bytes 1048576 | tf_op jit(solution)/shard_map/all_to_all | solution.py:216
  166.3 0.8 copy.16
  (6 shorter events, 0.1 us)
Async XLA Ops:
  6.5 36.7 %copy-start = (f32[16,128]{1,0:T(8,128)S(1)}, f32[16,128]{1,0:T(8,128)}, u32[]{:S(2)}) copy-start(f32[16,128]{1,0:T(8,128)} %param.7) | copy-start | bytes 24580
  8.4 5.4 %copy-start.4 = (bf16[128,2048]{1,0:T(8,128)(2,1)S(1)}, bf16[128,2048]{1,0:T(8,128)(2,1)}, u32[]{:S(2)}) copy-start(bf16[128,2048]{1,0:T(8,128)(2,1)} %param.5) | copy-start | bytes 1572868
  8.4 15.0 %all-to-all-start.2 = ((bf16[128,8,256]{2,0,1:T(8,128)(2,1)}), bf16[128,8,256]{2,0,1:T(8,128)(2,1)S(1)}, u32[]{:S(2)}, u32[]{:S(2)}) async-start(bf16[128,8,256]{2,0,1:T(8,128)(2,1)} %bitcast.23), calls=%async_computation.2 | async-start | bytes 1048576 | tf_op jit(solution)/shard_map/all_to_all | solution.py:184
  13.8 52.6 %all-gather.3.cloned.1.call-start = ((), (), s32[]{:S(2)}) async-start(), calls=%async_computation.4 | async-start | bytes 1310720 | tf_op jit(solution)/shard_map/all_gather | solution.py:199
  23.5 12.8 %copy-start.1 = (bf16[128,8,256]{2,0,1:T(8,128)(2,1)}, bf16[128,8,256]{2,0,1:T(8,128)(2,1)S(1)}, u32[]{:S(2)}) copy-start(bf16[128,8,256]{2,0,1:T(8,128)(2,1)S(1)} %all-to-all-done.2) | copy-start | bytes 1572868
  36.3 2.6 %copy-start.5 = (bf16[128,2048]{1,0:T(8,128)(2,1)S(1)}, bf16[128,2048]{1,0:T(8,128)(2,1)}, u32[]{:S(2)}) copy-start(bf16[128,2048]{1,0:T(8,128)(2,1)} %param.4) | copy-start | bytes 1572868
  39.7 28.2 %all-to-all-start = ((bf16[128,8,256]{2,0,1:T(8,128)(2,1)}), bf16[128,8,256]{2,0,1:T(8,128)(2,1)S(1)}, u32[]{:S(2)}, u32[]{:S(2)}) async-start(bf16[128,8,256]{2,0,1:T(8,128)(2,1)} %bitcast.25), calls=%async_computation | async-start | bytes 1048576 | tf_op jit(solution)/shard_map/all_to_all | solution.py:184
  66.4 1.5 copy-start.2
  66.4 1.5 copy-start.3
Sparse Core Ops, SparseCore 0:
  39.0 27.3 all-gather.2

commit v2 on v1

--- a/solution.py
+++ b/solution.py
@@ -11,6 +11,8 @@
 GROUP = 64
 EDGE = 32
 PACK = DK // EDGE
+STEP_PACKS = 2
+STEP_GROUPS = 4
 EPS = 1e-06
 F32 = jnp.float32
 BF16 = jnp.bfloat16
@@ -47,22 +49,37 @@
 def sweep_pack(rows, lane, sub):
     base = (lane // EDGE) * EDGE
     within = lane - base
-    for j in range(EDGE):
+
+    def take(block, pick):
+        return jnp.take_along_axis(block, pick, axis=1, mode="promise_in_bounds")
+
+    for j in range(0, EDGE, 2):
         at, inner = j // 8, j % 8
-        column = within == j
-        pick = base + j
-        pivot_row = jnp.broadcast_to(rows[at][inner : inner + 1, :], rows[at].shape)
-        pivot = jnp.take_along_axis(pivot_row, pick, axis=1, mode="promise_in_bounds")
-        scaled = jnp.where(column, -1.0, pivot_row) * (1.0 / pivot)
+        first, second = within == j, within == j + 1
+        either = jnp.logical_or(first, second)
+        pick1, pick2 = base + j, base + j + 1
+        row1 = jnp.broadcast_to(rows[at][inner : inner + 1, :], rows[at].shape)
+        row2 = jnp.broadcast_to(rows[at][inner + 1 : inner + 2, :], rows[at].shape)
+        a, b, d = take(row1, pick1), take(row1, pick2), take(row2, pick2)
+        inv1 = 1.0 / a
+        ratio = b * inv1
+        inv2 = 1.0 / (d - b * ratio)
+        scaled1 = jnp.where(first, -1.0, row1) * inv1
+        scaled2 = jnp.where(second, -1.0, jnp.where(first, 0.0, row2) - b * scaled1) * inv2
+        scaled1 = jnp.where(second, 0.0, scaled1)
         fresh = []
         for v, block in enumerate(rows):
-            col = jnp.take_along_axis(block, pick, axis=1, mode="promise_in_bounds")
-            gone = column
+            col1, col2 = take(block, pick1), take(block, pick2)
+            gone = either
             if v == at:
-                here = sub == inner
-                col = jnp.where(here, -1.0, col)
-                gone = jnp.logical_or(column, here)
-            fresh.append(jnp.where(gone, 0.0, block) - col * scaled)
+                here1, here2 = sub == inner, sub == inner + 1
+                col1 = jnp.where(here1, -1.0, col1)
+                col2 = jnp.where(here2, -1.0, jnp.where(here1, 0.0, col2) - col1 * ratio)
+                col1 = jnp.where(here2, 0.0, col1)
+                gone = jnp.logical_or(either, jnp.logical_or(here1, here2))
+            else:
+                col2 = col2 - col1 * ratio
+            fresh.append(jnp.where(gone, 0.0, block) - col1 * scaled1 - col2 * scaled2)
         rows = fresh
     return rows
 
@@ -105,20 +122,26 @@
         diag = lane32 - p * EDGE == sub32
         cleared = jnp.logical_or(row128 == p, lane128 == p)
 
-        def update(g, carry):
-            inverse = left_stack(split3(pinv_ref[g]))
-            for k in range(PACK):
-                s = g * PACK + k
-                rows = sys_ref[s, pl.ds(start, EDGE), :]
-                rows = jnp.where(mine, jnp.where(diag, -1.0, 0.0), rows)
-                parts = split3(rows)
-                full = dot(inverse, right_stack(parts), (0, 0))
-                scaled = full[k * EDGE : (k + 1) * EDGE, :]
-                change = dot(left_stack(parts), right_stack(split3(scaled)), (0, 0))
-                sys_ref[s] = jnp.where(cleared, 0.0, sys_ref[s]) + change
+        def update(turn, carry):
+            batch = [turn * STEP_PACKS + i for i in range(STEP_PACKS)]
+            rows, inverses = [], []
+            for g in batch:
+                inverses.append(jnp.transpose(left_stack(split3(pinv_ref[g]))))
+                for k in range(PACK):
+                    rows.append(sys_ref[g * PACK + k, pl.ds(start, EDGE), :])
+            rows = [split3(jnp.where(mine, jnp.where(diag, -1.0, 0.0), r)) for r in rows]
+            scaled = []
+            for i in range(STEP_PACKS):
+                for k in range(PACK):
+                    left = inverses[i][k * EDGE : (k + 1) * EDGE, :]
+                    scaled.append(dot(left, right_stack(rows[i * PACK + k]), (1, 0)))
+            change = [dot(left_stack(r), right_stack(split3(t)), (0, 0)) for r, t in zip(rows, scaled)]
+            for i, c in enumerate(change):
+                s = turn * STEP_PACKS * PACK + i
+                sys_ref[s] = jnp.where(cleared, 0.0, sys_ref[s]) + c
             return carry
 
-        return lax.fori_loop(0, packs, update, carry)
+        return lax.fori_loop(0, packs // STEP_PACKS, update, carry)
 
     lax.fori_loop(0, PACK, panel, 0)
 
@@ -131,42 +154,61 @@
         cols = slice(h * DK, (h + 1) * DK)
         ridge = jnp.where(eye, ridge_ref[h : h + 1, :], 0.0)
 
-        def step(c, run):
-            rows = pl.ds(pl.multiple_of(c * GROUP, GROUP), GROUP)
-            sys_ref[h * groups + c] = run[:, :DK] + ridge
-            vk_ref[h * groups + c] = run[:, DK:]
-            ku = ku_ref[rows, cols]
-            return run + dot(ku, jnp.concatenate([ku, v_ref[rows, cols]], axis=1), (0, 0))
-
-        lax.fori_loop(0, groups, step, pre_ref[h])
+        def step(turn, run):
+            adds = []
+            for i in range(STEP_GROUPS):
+                rows = pl.ds(pl.multiple_of((turn * STEP_GROUPS + i) * GROUP, GROUP), GROUP)
+                ku = ku_ref[rows, cols]
+                adds.append(dot(ku, jnp.concatenate([ku, v_ref[rows, cols]], axis=1), (0, 0)))
+            for i in range(STEP_GROUPS):
+                c = turn * STEP_GROUPS + i
+                sys_ref[h * groups + c] = run[:, :DK] + ridge
+                vk_ref[h * groups + c] = run[:, DK:]
+                run = run + adds[i]
+            return run
+
+        lax.fori_loop(0, groups // STEP_GROUPS, step, pre_ref[h])
 
 
 def finish(q_ref, ku_ref, v_ref, sys_ref, vk_ref, out_ref):
     groups = ku_ref.shape[0] // GROUP
     heads = ku_ref.shape[1] // DK
-    causal = lax.broadcasted_iota(jnp.int32, (GROUP, GROUP), 1) <= lax.broadcasted_iota(jnp.int32, (GROUP, GROUP), 0)
+    sub = lax.broadcasted_iota(jnp.int32, (GROUP, 2 * GROUP), 0)
+    lane = lax.broadcasted_iota(jnp.int32, (GROUP, 2 * GROUP), 1)
+    twice = lane >= GROUP
+    causal = jnp.where(twice, lane - GROUP, lane) <= sub
     for h in range(heads):
         cols = slice(h * DK, (h + 1) * DK)
 
-        def step(c, carry):
-            rows = pl.ds(pl.multiple_of(c * GROUP, GROUP), GROUP)
-            qu = unit(q_ref[rows, cols])
-            high, mid, low = split3(sys_ref[h * groups + c])
-            solved = -(dot(qu, high, (1, 0)) + (dot(qu, mid, (1, 0)) + dot(qu, low, (1, 0))))
-            shigh, smid, slow = split3(solved)
-            vhigh, vmid, vlow = split3(vk_ref[h * groups + c])
-            carried = dot(shigh, vhigh, (1, 0)) + (
-                dot(shigh, vmid, (1, 0)) + dot(smid, vhigh, (1, 0)) + (
-                    dot(smid, vmid, (1, 0)) + dot(shigh, vlow, (1, 0)) + dot(slow, vhigh, (1, 0))))
-            ku = ku_ref[rows, cols]
-            scores = dot(shigh, ku, (1, 1)) + (dot(smid, ku, (1, 1)) + dot(slow, ku, (1, 1)))
-            chigh, cmid, clow = split3(jnp.where(causal, scores, 0.0))
-            vb = v_ref[rows, cols]
-            inner = dot(chigh, vb, (1, 0)) + (dot(cmid, vb, (1, 0)) + dot(clow, vb, (1, 0)))
-            out_ref[rows, cols] = (carried + inner).astype(BF16)
+        def step(turn, carry):
+            places = [turn * STEP_GROUPS + i for i in range(STEP_GROUPS)]
+            rows = [pl.ds(pl.multiple_of(c * GROUP, GROUP), GROUP) for c in places]
+            solved = []
+            for c, r in zip(places, rows):
+                qu = unit(q_ref[r, cols])
+                full = jnp.concatenate(split3(sys_ref[h * groups + c]), axis=0)
+                solved.append(split3(-dot(jnp.concatenate([qu, qu, qu], axis=1), full, (1, 0))))
+            scores, carried = [], []
+            for c, r, (high, mid, low) in zip(places, rows, solved):
+                ku = ku_ref[r, cols]
+                ku = jnp.concatenate([ku, ku], axis=0)
+                ku = jnp.concatenate([ku, ku, ku], axis=1)
+                scores.append(dot(jnp.concatenate([high, mid, low], axis=1), ku, (1, 1)))
+                left = jnp.concatenate([high, high, mid, high, low, mid], axis=1)
+                carried.append(dot(left, right_stack(split3(vk_ref[h * groups + c])), (1, 0)))
+            results = []
+            for r, score, carry_in in zip(rows, scores, carried):
+                score = jnp.where(causal, score, 0.0)
+                high = score.astype(BF16).astype(F32)
+                both = jnp.where(twice, score - high, high).astype(BF16)
+                vb = v_ref[r, cols]
+                inner = dot(both, jnp.concatenate([vb, vb], axis=0), (1, 0))
+                results.append((carry_in + inner).astype(BF16))
+            for r, result in zip(rows, results):
+                out_ref[r, cols] = result
             return carry
 
-        lax.fori_loop(0, groups, step, 0)
+        lax.fori_loop(0, groups // STEP_GROUPS, step, 0)
 
 
 def solve_kernel(q_ref, ku_ref, v_ref, pre_ref, ridge_ref, out_ref, sys_ref, vk_ref, pinv_ref):

time: 174 us -> 124 us (0.71)
  Pallas kernels: 87.8 us -> 37.3 us
    pallas_call x1, Pallas kernels: 85.2 us -> 34.7 us  [body(): pl.pallas_call(solve_kernel, out_shape=jax.ShapeDtypeStruct((tokens, widt...]
  transfers between devices with their start and end apart: 3 -> 3, of which waited for: 2 -> 2; matrix products, arithmetic and copies ran while one was open for 1% -> 2% of each run, Pallas kernels for 0% -> 0%
where the time goes in v2:
time: 124 us; the launch traced here: 123 us
  Pallas kernels  37.3 us (30%)
  waiting for transfers between devices  32.7 us (26%)
  blocking collectives  25.9 us (21%)
  between operations  13.5 us (11%)
  starting transfers between devices  8.86 us (7%)
  local copies, waits for them, and re-layouts  3.64 us (3%)
  other arithmetic  1.48 us (1%)
    pallas_call x1, Pallas kernels, body(): pl.pallas_call(solve_kernel, out_shape=jax.ShapeDtypeStruct((tokens, widt...  34.7 us
    all_gather x1, waiting for transfers between devices, body(): gathered = lax.all_gather(total, 'seq')  23.1 us
    all_to_all x1, blocking collectives, body(): return lax.all_to_all(out, 'head', split_axis=0, concat_axis=1, tiled=True)  13.2 us
    all_to_all x1, blocking collectives, spread(): return lax.all_to_all(rows, 'head', split_axis=1, concat_axis=0, tiled=True)  12.8 us
    all_to_all x2, waiting for transfers between devices, spread(): return lax.all_to_all(rows, 'head', split_axis=1, concat_axis=0, tiled=True)  9.62 us
    all_to_all x2, starting transfers between devices, spread(): return lax.all_to_all(rows, 'head', split_axis=1, concat_axis=0, tiled=True)  8.82 us
    all_to_all x3, local copies, waits for them, and re-layouts, spread(): return lax.all_to_all(rows, 'head', split_axis=1, concat_axis=0, tiled=True)  2.74 us
    pallas_call x1, Pallas kernels, body(): pl.pallas_call(totals_kernel, out_shape=(jax.ShapeDtypeStruct((tokens, wi...  2.6 us
  transfers between devices with their start and end apart: 3, of which 2 were waited for; matrix products, arithmetic and copies ran while one was open for 2% of the time, Pallas kernels for 0%

profile of v2, /device:TPU:0, one launch (start us, length us, event | category | flops | bytes accessed | tf_op | source)
XLA Modules:
  0.0 123.5 jit_solution(6939497840357625317)
XLA Ops:
  6.5 0.0 copy-start
  6.5 1.9 %copy.20 = bf16[16,8,8,256]{3,2,0,1:T(8,128)(2,1)} copy(bf16[16,8,8,256]{3,2,1,0:T(8,128)(2,1)} %bitcast.34) | data formatting | bytes 1048576 | tf_op jit(solution)/shard_map/all_to_all | solution.py:226
  8.4 0.0 copy-start.4
  8.4 5.3 %all-to-all-start.2 = ((bf16[128,8,256]{2,0,1:T(8,128)(2,1)}), bf16[128,8,256]{2,0,1:T(8,128)(2,1)S(1)}, u32[]{:S(2)}, u32[]{:S(2)}) async-start(bf16[128,8,256]{2,0,1:T(8,128)(2,1)} %bitcast.23), calls=%async_computation.2 | async-start | bytes 1048576 | tf_op jit(solution)/shard_map/all_to_all | solution.py:226
  13.8 0.0 all-gather.3.cloned.1.call-start
  13.8 0.0 copy-done.4
  13.8 9.6 %all-to-all-done.2 = bf16[128,8,256]{2,0,1:T(8,128)(2,1)S(1)} async-done(((bf16[128,8,256]{2,0,1:T(8,128)(2,1)}), bf16[128,8,256]{2,0,1:T(8,128)(2,1)S(1)}, u32[]{:S(2)}, u32[]{:S(2)}) %all-to-all-start.2) | async-done | bytes 524320 | tf_op jit(solution)/shard_map/all_to_all | solution.py:226
  23.5 0.0 copy-start.1
  23.5 12.8 %all_to_all.76 = bf16[128,8,256]{2,0,1:T(8,128)(2,1)} all-to-all(bf16[128,8,256]{2,0,1:T(8,128)(2,1)S(1)} %bitcast.30), channel_id=1, replica_groups=mesh['seq'=4,'head'=8] {'head'}, dimensions={1} | all-to-all | bytes 1048576 | tf_op jit(solution)/shard_map/all_to_all | solution.py:226
  36.3 0.0 copy-done.1
  36.3 2.6 %shard_map.46 = (bf16[1024,256]{1,0:T(8,128)(2,1)}, f32[2,128,256]{2,1,0:T(8,128)}) custom-call(bf16[1024,256]{1,0:T(8,128)(2,1)} %bitcast.31, bf16[1024,256]{1,0:T(8,128)(2,1)} %bitcast.26), custom_call_target="tpu_custom_call" | custom-call | tf_op jit(solution)/shard_map/pallas_call | solution.py:232
  38.9 0.0 all-gather.3.cloned.1.call-update
  38.9 0.0 copy-done.5
  38.9 0.8 copy.22
  39.7 3.5 %all-to-all-start = ((bf16[128,8,256]{2,0,1:T(8,128)(2,1)}), bf16[128,8,256]{2,0,1:T(8,128)(2,1)S(1)}, u32[]{:S(2)}, u32[]{:S(2)}) async-start(bf16[128,8,256]{2,0,1:T(8,128)(2,1)} %bitcast.25), calls=%async_computation | async-start | bytes 1048576 | tf_op jit(solution)/shard_map/all_to_all | solution.py:226
  43.2 0.0 copy-done
  43.3 23.1 %all-gather.3.cloned.1.call-done = f32[8,128,256]{2,1,0:T(8,128)} async-done(((f32[2,128,256]{2,1,0:T(8,128)}), f32[8,128,256]{2,1,0:T(8,128)}) %all-gather.3.cloned.1.call-update) | async-done | bytes 1048592 | tf_op jit(solution)/shard_map/all_gather | solution.py:241
  66.4 1.5 %select_reduce_fusion.pre_ref = f32[2,128,256]{2,1,0:T(8,128)S(1)} fusion(f32[4,2,128,256]{3,2,1,0:T(8,128)} %bitcast.33, pred[4]{0:T(512)(128)(4,1)S(1)} %iota_compare_fusion), kind=kLoop, calls=%fused_computation | loop fusion | flops 458752 | bytes 1310724 | tf_op jit(solution)/shard_map/reduce_sum | solution.py:244
  67.9 0.0 all-to-all-done
  67.9 0.0 copy-done.2
  67.9 0.0 copy-done.3
  67.9 34.7 %shard_map.47 = bf16[1024,256]{1,0:T(8,128)(2,1)S(1)} custom-call(bf16[1024,256]{1,0:T(8,128)(2,1)S(1)} %bitcast.28, bf16[1024,256]{1,0:T(8,128)(2,1)S(1)} %copy-done.3, bf16[1024,256]{1,0:T(8,128)(2,1)S(1)} %bitcast.27, f32[2,128,256]{2,1,0:T(8,128)S(1)} %select_reduce_fusion.pre_ref, f32[2,128]{1,0:T(2,128)S(1)} %constant_dynamic-slice_fusion.ridge_ref), custom_call_target="tpu_custom_call" | custom-call | tf_op jit(solution)/shard_map/pallas_call | solution.py:246
  102.6 13.2 %all_to_all.77 = bf16[8,128,256]{2,1,0:T(8,128)(2,1)S(1)} all-to-all(bf16[8,128,256]{2,1,0:T(8,128)(2,1)S(1)} %bitcast.29), channel_id=1, replica_groups=mesh['seq'=4,'head'=8] {'head'}, dimensions={0} | all-to-all | bytes 1048576 | tf_op jit(solution)/shard_map/all_to_all | solution.py:258
  115.8 0.8 copy.16
  (6 shorter events, 0.1 us)
Async XLA Ops:
  6.5 36.7 %copy-start = (f32[16,128]{1,0:T(8,128)S(1)}, f32[16,128]{1,0:T(8,128)}, u32[]{:S(2)}) copy-start(f32[16,128]{1,0:T(8,128)} %param.7) | copy-start | bytes 24580
  8.4 5.4 %copy-start.4 = (bf16[128,2048]{1,0:T(8,128)(2,1)S(1)}, bf16[128,2048]{1,0:T(8,128)(2,1)}, u32[]{:S(2)}) copy-start(bf16[128,2048]{1,0:T(8,128)(2,1)} %param.5) | copy-start | bytes 1572868
  8.4 15.0 %all-to-all-start.2 = ((bf16[128,8,256]{2,0,1:T(8,128)(2,1)}), bf16[128,8,256]{2,0,1:T(8,128)(2,1)S(1)}, u32[]{:S(2)}, u32[]{:S(2)}) async-start(bf16[128,8,256]{2,0,1:T(8,128)(2,1)} %bitcast.23), calls=%async_computation.2 | async-start | bytes 1048576 | tf_op jit(solution)/shard_map/all_to_all | solution.py:226
  13.8 52.6 %all-gather.3.cloned.1.call-start = ((), (), s32[]{:S(2)}) async-start(), calls=%async_computation.4 | async-start | bytes 1310720 | tf_op jit(solution)/shard_map/all_gather | solution.py:241
  23.5 12.8 %copy-start.1 = (bf16[128,8,256]{2,0,1:T(8,128)(2,1)}, bf16[128,8,256]{2,0,1:T(8,128)(2,1)S(1)}, u32[]{:S(2)}) copy-start(bf16[128,8,256]{2,0,1:T(8,128)(2,1)S(1)} %all-to-all-done.2) | copy-start | bytes 1572868
  36.3 2.6 %copy-start.5 = (bf16[128,2048]{1,0:T(8,128)(2,1)S(1)}, bf16[128,2048]{1,0:T(8,128)(2,1)}, u32[]{:S(2)}) copy-start(bf16[128,2048]{1,0:T(8,128)(2,1)} %param.4) | copy-start | bytes 1572868
  39.7 28.2 %all-to-all-start = ((bf16[128,8,256]{2,0,1:T(8,128)(2,1)}), bf16[128,8,256]{2,0,1:T(8,128)(2,1)S(1)}, u32[]{:S(2)}, u32[]{:S(2)}) async-start(bf16[128,8,256]{2,0,1:T(8,128)(2,1)} %bitcast.25), calls=%async_computation | async-start | bytes 1048576 | tf_op jit(solution)/shard_map/all_to_all | solution.py:226
  66.4 1.5 %copy-start.2 = (bf16[128,8,256]{2,0,1:T(8,128)(2,1)S(1)}, bf16[128,8,256]{2,0,1:T(8,128)(2,1)}, u32[]{:S(2)}) copy-start(bf16[128,8,256]{2,0,1:T(8,128)(2,1)} %copy-done.1) | copy-start | bytes 1572868
  66.4 1.5 %copy-start.3 = (bf16[1024,256]{1,0:T(8,128)(2,1)S(1)}, bf16[1024,256]{1,0:T(8,128)(2,1)}, u32[]{:S(2)}) copy-start(bf16[1024,256]{1,0:T(8,128)(2,1)} %get-tuple-element.7.ku_ref) | copy-start | bytes 1572868
Sparse Core Ops, SparseCore 0:
  39.0 27.3 all-gather.2

commit v3 on v2

--- a/solution.py
+++ b/solution.py
@@ -84,16 +84,6 @@
     return rows
 
 
-def totals_kernel(k_ref, v_ref, ku_ref, tot_ref):
-    heads = k_ref.shape[1] // DK
-    for h in range(heads):
-        cols = slice(h * DK, (h + 1) * DK)
-        ku = unit(k_ref[:, cols])
-        ku_ref[:, cols] = ku
-        both = jnp.concatenate([ku, v_ref[:, cols]], axis=1)
-        tot_ref[h] = dot(ku, both, (0, 0))
-
-
 def invert_all(sys_ref, pinv_ref):
     count = sys_ref.shape[0]
     packs = count // PACK
@@ -146,116 +136,274 @@
     lax.fori_loop(0, PACK, panel, 0)
 
 
-def build_systems(ku_ref, v_ref, pre_ref, ridge_ref, sys_ref, vk_ref):
-    groups = ku_ref.shape[0] // GROUP
-    heads = ku_ref.shape[1] // DK
+def whole_kernel(
+    owners, shards, q_hbm, k_hbm, v_hbm, ridge_ref, out_hbm,
+    q_all, k_all, v_all, sys_ref, vk_ref, pinv_ref, stage, gram_total, vk_total, gram_slots, vk_slots,
+    send_sems, recv_sems, local_sems, out_send, out_recv, out_local, gram_send, gram_recv, vk_send, vk_recv,
+):
+    me, shard = lax.axis_index("head"), lax.axis_index("seq")
+    rows_each = q_hbm.shape[0]
+    width = q_all.shape[1]
+    heads = width // DK
+    per_source = rows_each // GROUP
+    groups = owners * per_source
+    moved = ((k_hbm, k_all), (v_hbm, v_all), (q_hbm, q_all))
+
+    def rows_of(source):
+        return pl.ds(pl.multiple_of(source * rows_each, rows_each), rows_each)
+
+    def cols_of(owner):
+        return pl.ds(pl.multiple_of(owner * width, width), width)
+
+    def incoming(kind, source):
+        return pltpu.make_async_remote_copy(
+            src_ref=moved[kind][0].at[:, cols_of(source)],
+            dst_ref=moved[kind][1].at[rows_of(source), :],
+            send_sem=send_sems.at[kind, source],
+            recv_sem=recv_sems.at[kind, source],
+            device_id={"head": source},
+            device_id_type=pl.DeviceIdType.MESH,
+        )
+
+    def outgoing(kind, peer):
+        return pltpu.make_async_remote_copy(
+            src_ref=moved[kind][0].at[:, cols_of(peer)],
+            dst_ref=moved[kind][1].at[rows_of(me), :],
+            send_sem=send_sems.at[kind, peer],
+            recv_sem=recv_sems.at[kind, me],
+            device_id={"head": peer},
+            device_id_type=pl.DeviceIdType.MESH,
+        )
+
+    def own(kind):
+        return pltpu.make_async_copy(
+            moved[kind][0].at[:, cols_of(me)], moved[kind][1].at[rows_of(me), :], local_sems.at[kind]
+        )
+
+    def total_copy(total, slots, send, recv, far, target):
+        return pltpu.make_async_remote_copy(
+            src_ref=total,
+            dst_ref=slots.at[far - 1],
+            send_sem=send.at[far - 1],
+            recv_sem=recv.at[far - 1],
+            device_id={"seq": target},
+            device_id_type=pl.DeviceIdType.MESH,
+        )
+
+    def send_totals(total, slots, send, recv):
+        for far in range(1, shards):
+            @pl.when(shard + far < shards)
+            def _():
+                total_copy(total, slots, send, recv, far, shard + far).start()
+
+    def wait_totals(total, slots, send, recv):
+        for far in range(1, shards):
+            @pl.when(shard - far >= 0)
+            def _():
+                total_copy(total, slots, send, recv, far, shard - far).wait_recv()
+
+    def drain_totals(total, slots, send, recv):
+        for far in range(1, shards):
+            @pl.when(shard + far < shards)
+            def _():
+                total_copy(total, slots, send, recv, far, shard + far).wait_send()
+
+    barrier = pltpu.get_barrier_semaphore()
+    for step in range(1, owners):
+        pl.semaphore_signal(barrier, inc=1, device_id={"head": lax.rem(me + step, owners)}, device_id_type=pl.DeviceIdType.MESH)
+    for step in range(1, shards):
+        pl.semaphore_signal(barrier, inc=1, device_id={"seq": lax.rem(shard + step, shards)}, device_id_type=pl.DeviceIdType.MESH)
+    for kind in range(3):
+        own(kind).start()
+    pl.semaphore_wait(barrier, owners + shards - 2)
+    for kind in range(3):
+        for step in range(1, owners):
+            outgoing(kind, lax.rem(me + step, owners)).start()
+    for kind in range(3):
+        own(kind).wait()
+
     eye = lax.broadcasted_iota(jnp.int32, (DK, DK), 0) == lax.broadcasted_iota(jnp.int32, (DK, DK), 1)
+    ridges = [jnp.where(eye, ridge_ref[pl.ds(me * heads + h, 1), :], 0.0) for h in range(heads)]
+
+    def rows_in(source, i):
+        return pl.ds(pl.multiple_of(source * rows_each + i * GROUP, GROUP), GROUP)
+
+    def keys_in(source, runs):
+        @pl.when(source != me)
+        def _():
+            incoming(0, source).wait_recv()
+
+        adds = []
+        for h in range(heads):
+            for i in range(per_source):
+                ku = unit(k_all[rows_in(source, i), h * DK : (h + 1) * DK])
+                k_all[rows_in(source, i), h * DK : (h + 1) * DK] = ku
+                adds.append(dot(ku, ku, (0, 0)))
+        runs = list(runs)
+        for h in range(heads):
+            for i in range(per_source):
+                sys_ref[h * groups + source * per_source + i] = runs[h] + ridges[h]
+                runs[h] = runs[h] + adds[h * per_source + i]
+        return tuple(runs)
+
+    zero = tuple(jnp.zeros((DK, DK), F32) for _ in range(heads))
+    runs = lax.fori_loop(0, owners, keys_in, zero)
     for h in range(heads):
-        cols = slice(h * DK, (h + 1) * DK)
-        ridge = jnp.where(eye, ridge_ref[h : h + 1, :], 0.0)
-
-        def step(turn, run):
-            adds = []
-            for i in range(STEP_GROUPS):
-                rows = pl.ds(pl.multiple_of((turn * STEP_GROUPS + i) * GROUP, GROUP), GROUP)
-                ku = ku_ref[rows, cols]
-                adds.append(dot(ku, jnp.concatenate([ku, v_ref[rows, cols]], axis=1), (0, 0)))
-            for i in range(STEP_GROUPS):
-                c = turn * STEP_GROUPS + i
-                sys_ref[h * groups + c] = run[:, :DK] + ridge
-                vk_ref[h * groups + c] = run[:, DK:]
-                run = run + adds[i]
-            return run
-
-        lax.fori_loop(0, groups // STEP_GROUPS, step, pre_ref[h])
-
-
-def finish(q_ref, ku_ref, v_ref, sys_ref, vk_ref, out_ref):
-    groups = ku_ref.shape[0] // GROUP
-    heads = ku_ref.shape[1] // DK
+        gram_total[h] = runs[h]
+    send_totals(gram_total, gram_slots, gram_send, gram_recv)
+
+    def values_in(source, runs):
+        @pl.when(source != me)
+        def _():
+            incoming(1, source).wait_recv()
+
+        adds = []
+        for h in range(heads):
+            for i in range(per_source):
+                cols = slice(h * DK, (h + 1) * DK)
+                adds.append(dot(k_all[rows_in(source, i), cols], v_all[rows_in(source, i), cols], (0, 0)))
+        runs = list(runs)
+        for h in range(heads):
+            for i in range(per_source):
+                vk_ref[h * groups + source * per_source + i] = runs[h]
+                runs[h] = runs[h] + adds[h * per_source + i]
+        return tuple(runs)
+
+    runs = lax.fori_loop(0, owners, values_in, zero)
+    for h in range(heads):
+        vk_total[h] = runs[h]
+    send_totals(vk_total, vk_slots, vk_send, vk_recv)
+
+    def sum_slots(slots, total):
+        for h in range(heads):
+            total[h] = jnp.zeros((DK, DK), F32)
+        for far in range(1, shards):
+            @pl.when(shard - far >= 0)
+            def _():
+                for h in range(heads):
+                    total[h] = total[h] + slots[far - 1, h]
+
+    wait_totals(gram_total, gram_slots, gram_send, gram_recv)
+    drain_totals(gram_total, gram_slots, gram_send, gram_recv)
+    sum_slots(gram_slots, gram_total)
+    for h in range(heads):
+        extra = gram_total[h]
+
+        def add(c, carry):
+            sys_ref[h * groups + c] = sys_ref[h * groups + c] + extra
+            return carry
+
+        lax.fori_loop(0, groups, add, 0)
+
+    invert_all(sys_ref, pinv_ref)
+
+    wait_totals(vk_total, vk_slots, vk_send, vk_recv)
+    drain_totals(vk_total, vk_slots, vk_send, vk_recv)
+    sum_slots(vk_slots, vk_total)
+    for step in range(1, owners):
+        incoming(2, lax.rem(me + step, owners)).wait_recv()
+
+    def result_copy(peer):
+        return pltpu.make_async_remote_copy(
+            src_ref=stage.at[peer],
+            dst_ref=out_hbm.at[:, cols_of(me)],
+            send_sem=out_send.at[peer],
+            recv_sem=out_recv.at[me],
+            device_id={"head": peer},
+            device_id_type=pl.DeviceIdType.MESH,
+        )
+
     sub = lax.broadcasted_iota(jnp.int32, (GROUP, 2 * GROUP), 0)
     lane = lax.broadcasted_iota(jnp.int32, (GROUP, 2 * GROUP), 1)
     twice = lane >= GROUP
     causal = jnp.where(twice, lane - GROUP, lane) <= sub
-    for h in range(heads):
-        cols = slice(h * DK, (h + 1) * DK)
-
-        def step(turn, carry):
-            places = [turn * STEP_GROUPS + i for i in range(STEP_GROUPS)]
-            rows = [pl.ds(pl.multiple_of(c * GROUP, GROUP), GROUP) for c in places]
-            solved = []
-            for c, r in zip(places, rows):
-                qu = unit(q_ref[r, cols])
-                full = jnp.concatenate(split3(sys_ref[h * groups + c]), axis=0)
-                solved.append(split3(-dot(jnp.concatenate([qu, qu, qu], axis=1), full, (1, 0))))
-            scores, carried = [], []
-            for c, r, (high, mid, low) in zip(places, rows, solved):
-                ku = ku_ref[r, cols]
-                ku = jnp.concatenate([ku, ku], axis=0)
-                ku = jnp.concatenate([ku, ku, ku], axis=1)
-                scores.append(dot(jnp.concatenate([high, mid, low], axis=1), ku, (1, 1)))
-                left = jnp.concatenate([high, high, mid, high, low, mid], axis=1)
-                carried.append(dot(left, right_stack(split3(vk_ref[h * groups + c])), (1, 0)))
-            results = []
-            for r, score, carry_in in zip(rows, scores, carried):
-                score = jnp.where(causal, score, 0.0)
-                high = score.astype(BF16).astype(F32)
-                both = jnp.where(twice, score - high, high).astype(BF16)
-                vb = v_ref[r, cols]
-                inner = dot(both, jnp.concatenate([vb, vb], axis=0), (1, 0))
-                results.append((carry_in + inner).astype(BF16))
-            for r, result in zip(rows, results):
-                out_ref[r, cols] = result
-            return carry
-
-        lax.fori_loop(0, groups // STEP_GROUPS, step, 0)
-
-
-def solve_kernel(q_ref, ku_ref, v_ref, pre_ref, ridge_ref, out_ref, sys_ref, vk_ref, pinv_ref):
-    build_systems(ku_ref, v_ref, pre_ref, ridge_ref, sys_ref, vk_ref)
-    invert_all(sys_ref, pinv_ref)
-    finish(q_ref, ku_ref, v_ref, sys_ref, vk_ref, out_ref)
+
+    def finish(step, carry):
+        source = lax.rem(me + 1 + step, owners)
+        jobs = [(h, i) for h in range(heads) for i in range(per_source)]
+        solved = []
+        for h, i in jobs:
+            qu = unit(q_all[rows_in(source, i), h * DK : (h + 1) * DK])
+            full = jnp.concatenate(split3(sys_ref[h * groups + source * per_source + i]), axis=0)
+            solved.append(split3(-dot(jnp.concatenate([qu, qu, qu], axis=1), full, (1, 0))))
+        scores, carried = [], []
+        for (h, i), (high, mid, low) in zip(jobs, solved):
+            ku = k_all[rows_in(source, i), h * DK : (h + 1) * DK]
+            ku = jnp.concatenate([ku, ku], axis=0)
+            ku = jnp.concatenate([ku, ku, ku], axis=1)
+            scores.append(dot(jnp.concatenate([high, mid, low], axis=1), ku, (1, 1)))
+            left = jnp.concatenate([high, high, mid, high, low, mid], axis=1)
+            start = vk_ref[h * groups + source * per_source + i] + vk_total[h]
+            carried.append(dot(left, right_stack(split3(start)), (1, 0)))
+        for (h, i), score, carry_in in zip(jobs, scores, carried):
+            score = jnp.where(causal, score, 0.0)
+            high = score.astype(BF16).astype(F32)
+            both = jnp.where(twice, score - high, high).astype(BF16)
+            vb = v_all[rows_in(source, i), h * DK : (h + 1) * DK]
+            inner = dot(both, jnp.concatenate([vb, vb], axis=0), (1, 0))
+            stage[source, i * GROUP : (i + 1) * GROUP, h * DK : (h + 1) * DK] = (carry_in + inner).astype(BF16)
+
+        @pl.when(source != me)
+        def _():
+            result_copy(source).start()
+
+        return carry
+
+    lax.fori_loop(0, owners, finish, 0)
+    mine = pltpu.make_async_copy(stage.at[me], out_hbm.at[:, cols_of(me)], out_local)
+    mine.start()
+    for step in range(1, owners):
+        peer = lax.rem(me + step, owners)
+        for kind in range(3):
+            outgoing(kind, peer).wait_send()
+        result_copy(peer).wait_send()
+    for step in range(1, owners):
+        source = lax.rem(me + step, owners)
+        pltpu.make_async_remote_copy(
+            src_ref=stage.at[source],
+            dst_ref=out_hbm.at[:, cols_of(source)],
+            send_sem=out_send.at[source],
+            recv_sem=out_recv.at[source],
+            device_id={"head": source},
+            device_id_type=pl.DeviceIdType.MESH,
+        ).wait_recv()
+    mine.wait()
 
 
 def body(queries, key_rows, value_rows, ridge_diag):
-    owners = lax.axis_size("head")
-    heads = queries.shape[1] // DK // owners
-    width = heads * DK
-
-    def spread(rows):
-        return lax.all_to_all(rows, "head", split_axis=1, concat_axis=0, tiled=True)
-
-    k_all, v_all, q_all = spread(key_rows), spread(value_rows), spread(queries)
-    tokens = k_all.shape[0]
+    owners, shards = lax.axis_size("head"), lax.axis_size("seq")
+    rows, columns = queries.shape
+    width = columns // owners
+    heads = width // DK
+    tokens = rows * owners
     systems = heads * (tokens // GROUP)
-    vmem = pl.BlockSpec(memory_space=pltpu.VMEM)
-    ku, total = pl.pallas_call(
-        totals_kernel,
-        out_shape=(
-            jax.ShapeDtypeStruct((tokens, width), BF16),
-            jax.ShapeDtypeStruct((heads, DK, 2 * DK), F32),
-        ),
-        in_specs=[vmem] * 2,
-        out_specs=(vmem, vmem),
-    )(k_all, v_all)
-    gathered = lax.all_gather(total, "seq")
-    mine = lax.axis_index("seq")
-    before = jnp.arange(lax.axis_size("seq")) < mine
-    pre = jnp.sum(jnp.where(before[:, None, None, None], gathered, 0.0), axis=0)
-    ridge = lax.dynamic_slice_in_dim(ridge_diag, lax.axis_index("head") * heads, heads, 0)
-    out = pl.pallas_call(
-        solve_kernel,
-        out_shape=jax.ShapeDtypeStruct((tokens, width), BF16),
-        in_specs=[vmem] * 5,
-        out_specs=vmem,
+    anywhere = pl.BlockSpec(memory_space=pl.ANY)
+    dma = pltpu.SemaphoreType.DMA
+    return pl.pallas_call(
+        functools.partial(whole_kernel, owners, shards),
+        out_shape=jax.ShapeDtypeStruct((rows, columns), BF16),
+        in_specs=[anywhere] * 3 + [pl.BlockSpec(memory_space=pltpu.VMEM)],
+        out_specs=anywhere,
         scratch_shapes=[
+            pltpu.VMEM((tokens, width), BF16),
+            pltpu.VMEM((tokens, width), BF16),
+            pltpu.VMEM((tokens, width), BF16),
             pltpu.VMEM((systems, DK, DK), F32),
             pltpu.VMEM((systems, DK, DK), F32),
             pltpu.VMEM((systems // PACK, EDGE, DK), F32),
+            pltpu.VMEM((owners, rows, width), BF16),
+            pltpu.VMEM((heads, DK, DK), F32),
+            pltpu.VMEM((heads, DK, DK), F32),
+            pltpu.VMEM((shards - 1, heads, DK, DK), F32),
+            pltpu.VMEM((shards - 1, heads, DK, DK), F32),
+            dma((3, owners)), dma((3, owners)), dma((3,)),
+            dma((owners,)), dma((owners,)), dma,
+            dma((shards - 1,)), dma((shards - 1,)), dma((shards - 1,)), dma((shards - 1,)),
         ],
-        compiler_params=pltpu.CompilerParams(vmem_limit_bytes=48 * 1024 * 1024),
-    )(q_all, ku, v_all, pre, ridge)
-    return lax.all_to_all(out, "head", split_axis=0, concat_axis=1, tiled=True)
+        compiler_params=pltpu.CompilerParams(
+            vmem_limit_bytes=48 * 1024 * 1024, collective_id=0, has_side_effects=True
+        ),
+    )(queries, key_rows, value_rows, ridge_diag)
 
 
 def solution(mesh):

time: 124 us -> 74.5 us (0.60)
  the two profiles are of different devices: /device:TPU:0 before, /device:TPU:27 now
where the time goes in v3:
time: 74.5 us; the launch traced here: 74.2 us
  Pallas kernels  69.5 us (93%)
  local copies, waits for them, and re-layouts  4.62 us (6%)
    pallas_call x1, Pallas kernels, body(): pl.pallas_call(functools.partial(whole_kernel, owners, shards), out_shape...  69.5 us
    unnamed x9, local copies, waits for them, and re-layouts  4.62 us

profile of v3, /device:TPU:27, one launch (start us, length us, event | category | flops | bytes accessed | tf_op | source)
XLA Modules:
  0.0 74.2 jit_solution(1344181071628338480)
XLA Ops:
  0.0 0.0 copy-start
  0.0 1.0 %copy-done = bf16[128,2048]{1,0:T(8,128)(2,1)S(1)} copy-done((bf16[128,2048]{1,0:T(8,128)(2,1)S(1)}, bf16[128,2048]{1,0:T(8,128)(2,1)}, u32[]{:S(2)}) %copy-start) | copy-done | bytes 524312
  1.0 0.0 copy-start.1
  1.0 1.0 %copy-done.1 = bf16[128,2048]{1,0:T(8,128)(2,1)S(1)} copy-done((bf16[128,2048]{1,0:T(8,128)(2,1)S(1)}, bf16[128,2048]{1,0:T(8,128)(2,1)}, u32[]{:S(2)}) %copy-start.1) | copy-done | bytes 524312
  2.1 0.0 copy-start.2
  2.1 1.0 %copy-done.2 = bf16[128,2048]{1,0:T(8,128)(2,1)S(1)} copy-done((bf16[128,2048]{1,0:T(8,128)(2,1)S(1)}, bf16[128,2048]{1,0:T(8,128)(2,1)}, u32[]{:S(2)}) %copy-start.2) | copy-done | bytes 524312
  3.1 0.0 copy-start.3
  3.1 0.7 copy-done.3
  3.8 69.5 %shard_map.46 = bf16[128,2048]{1,0:T(8,128)(2,1)S(1)} custom-call(bf16[128,2048]{1,0:T(8,128)(2,1)S(1)} %copy-done, bf16[128,2048]{1,0:T(8,128)(2,1)S(1)} %copy-done.1, bf16[128,2048]{1,0:T(8,128)(2,1)S(1)} %copy-done.2, f32[16,128]{1,0:T(8,128)S(1)} %copy-done.3), custom_call_target="tpu_custom_call" | custom-call | tf_op jit(solution)/shard_map/pallas_call | solution.py:382
  73.4 0.8 %copy.6 = bf16[128,2048]{1,0:T(8,128)(2,1)} copy(bf16[128,2048]{1,0:T(8,128)(2,1)S(1)} %shard_map.46) | data formatting | bytes 1048576
Async XLA Ops:
  0.0 1.0 %copy-start = (bf16[128,2048]{1,0:T(8,128)(2,1)S(1)}, bf16[128,2048]{1,0:T(8,128)(2,1)}, u32[]{:S(2)}) copy-start(bf16[128,2048]{1,0:T(8,128)(2,1)} %q_hbm.1) | copy-start | bytes 1572868
  1.0 1.0 %copy-start.1 = (bf16[128,2048]{1,0:T(8,128)(2,1)S(1)}, bf16[128,2048]{1,0:T(8,128)(2,1)}, u32[]{:S(2)}) copy-start(bf16[128,2048]{1,0:T(8,128)(2,1)} %k_hbm.1) | copy-start | bytes 1572868
  2.1 1.0 %copy-start.2 = (bf16[128,2048]{1,0:T(8,128)(2,1)S(1)}, bf16[128,2048]{1,0:T(8,128)(2,1)}, u32[]{:S(2)}) copy-start(bf16[128,2048]{1,0:T(8,128)(2,1)} %v_hbm.1) | copy-start | bytes 1572868
  3.1 0.7 copy-start.3

commit v4 on v3

--- a/solution.py
+++ b/solution.py
@@ -11,8 +11,7 @@
 GROUP = 64
 EDGE = 32
 PACK = DK // EDGE
-STEP_PACKS = 2
-STEP_GROUPS = 4
+STEP_PACKS = 4
 EPS = 1e-06
 F32 = jnp.float32
 BF16 = jnp.bfloat16
@@ -46,42 +45,41 @@
     return jnp.concatenate([high, mid, high, low, high, mid], axis=0)
 
 
-def sweep_pack(rows, lane, sub):
+def sweep_round(rows, lane, sub, turn):
     base = (lane // EDGE) * EDGE
     within = lane - base
 
     def take(block, pick):
         return jnp.take_along_axis(block, pick, axis=1, mode="promise_in_bounds")
 
-    for j in range(0, EDGE, 2):
-        at, inner = j // 8, j % 8
-        first, second = within == j, within == j + 1
-        either = jnp.logical_or(first, second)
-        pick1, pick2 = base + j, base + j + 1
-        row1 = jnp.broadcast_to(rows[at][inner : inner + 1, :], rows[at].shape)
-        row2 = jnp.broadcast_to(rows[at][inner + 1 : inner + 2, :], rows[at].shape)
-        a, b, d = take(row1, pick1), take(row1, pick2), take(row2, pick2)
-        inv1 = 1.0 / a
-        ratio = b * inv1
-        inv2 = 1.0 / (d - b * ratio)
-        scaled1 = jnp.where(first, -1.0, row1) * inv1
-        scaled2 = jnp.where(second, -1.0, jnp.where(first, 0.0, row2) - b * scaled1) * inv2
-        scaled1 = jnp.where(second, 0.0, scaled1)
-        fresh = []
-        for v, block in enumerate(rows):
-            col1, col2 = take(block, pick1), take(block, pick2)
-            gone = either
-            if v == at:
-                here1, here2 = sub == inner, sub == inner + 1
-                col1 = jnp.where(here1, -1.0, col1)
-                col2 = jnp.where(here2, -1.0, jnp.where(here1, 0.0, col2) - col1 * ratio)
-                col1 = jnp.where(here2, 0.0, col1)
-                gone = jnp.logical_or(either, jnp.logical_or(here1, here2))
-            else:
-                col2 = col2 - col1 * ratio
-            fresh.append(jnp.where(gone, 0.0, block) - col1 * scaled1 - col2 * scaled2)
-        rows = fresh
-    return rows
+    j = turn
+    at, inner = j // 8, j % 8
+    first, second = within == j, within == j + 1
+    either = jnp.logical_or(first, second)
+    pick1, pick2 = base + j, base + j + 1
+    row1 = jnp.broadcast_to(rows[at][inner : inner + 1, :], rows[at].shape)
+    row2 = jnp.broadcast_to(rows[at][inner + 1 : inner + 2, :], rows[at].shape)
+    a, b, d = take(row1, pick1), take(row1, pick2), take(row2, pick2)
+    inv1 = 1.0 / a
+    ratio = b * inv1
+    inv2 = 1.0 / (d - b * ratio)
+    scaled1 = jnp.where(first, -1.0, row1) * inv1
+    scaled2 = jnp.where(second, -1.0, jnp.where(first, 0.0, row2) - b * scaled1) * inv2
+    scaled1 = jnp.where(second, 0.0, scaled1)
+    fresh = []
+    for v, block in enumerate(rows):
+        col1, col2 = take(block, pick1), take(block, pick2)
+        gone = either
+        if v == at:
+            here1, here2 = sub == inner, sub == inner + 1
+            col1 = jnp.where(here1, -1.0, col1)
+            col2 = jnp.where(here2, -1.0, jnp.where(here1, 0.0, col2) - col1 * ratio)
+            col1 = jnp.where(here2, 0.0, col1)
+            gone = jnp.logical_or(either, jnp.logical_or(here1, here2))
+        else:
+            col2 = col2 - col1 * ratio
+        fresh.append(jnp.where(gone, 0.0, block) - col1 * scaled1 - col2 * scaled2)
+    return fresh
 
 
 def invert_all(sys_ref, pinv_ref):
@@ -104,9 +102,10 @@
                 piece = pltpu.roll(piece, lax.rem((k - p) * EDGE + DK, DK), 1)
                 packed = piece if packed is None else jnp.where(lane32 // EDGE == k, piece, packed)
             all_rows.append([packed[8 * v : 8 * v + 8, :] for v in range(EDGE // 8)])
+        for turn in range(0, EDGE, 2):
+            all_rows = [sweep_round(rows, lane, sub, turn) for rows in all_rows]
         for g in range(packs):
-            done = sweep_pack(all_rows[g], lane, sub)
-            pinv_ref[g] = jnp.concatenate(done, axis=0)
+            pinv_ref[g] = jnp.concatenate(all_rows[g], axis=0)
 
         mine = lane32 // EDGE == p
         diag = lane32 - p * EDGE == sub32
@@ -191,7 +190,7 @@
         )
 
     def send_totals(total, slots, send, recv):
-        for far in range(1, shards):
+        for far in reversed(range(1, shards)):
             @pl.when(shard + far < shards)
             def _():
                 total_copy(total, slots, send, recv, far, shard + far).start()
@@ -377,7 +376,7 @@
     heads = width // DK
     tokens = rows * owners
     systems = heads * (tokens // GROUP)
-    anywhere = pl.BlockSpec(memory_space=pl.ANY)
+    anywhere = pl.BlockSpec(memory_space=pltpu.HBM)
     dma = pltpu.SemaphoreType.DMA
     return pl.pallas_call(
         functools.partial(whole_kernel, owners, shards),
@@ -401,7 +400,7 @@
             dma((shards - 1,)), dma((shards - 1,)), dma((shards - 1,)), dma((shards - 1,)),
         ],
         compiler_params=pltpu.CompilerParams(
-            vmem_limit_bytes=48 * 1024 * 1024, collective_id=0, has_side_effects=True
+            vmem_limit_bytes=67_000_000, collective_id=0, has_side_effects=True
         ),
     )(queries, key_rows, value_rows, ridge_diag)
 

time: 74.5 us -> 62.9 us (0.84)
  the two profiles are of different devices: /device:TPU:27 before, /device:TPU:19 now
where the time goes in v4:
time: 62.9 us; the launch traced here: 62.7 us
  Pallas kernels  60.8 us (97%)
  local copies, waits for them, and re-layouts  1.88 us (3%)
    pallas_call x1, Pallas kernels, body(): pl.pallas_call(functools.partial(whole_kernel, owners, shards), out_shape...  60.8 us
    unnamed x1, local copies, waits for them, and re-layouts  1.88 us

profile of v4, /device:TPU:19, one launch (start us, length us, event | category | flops | bytes accessed | tf_op | source)
XLA Modules:
  0.0 62.7 jit_solution(17099845858979625109)
XLA Ops:
  0.0 60.8 %shard_map.46 = bf16[128,2048]{1,0:T(8,128)(2,1)} custom-call(bf16[128,2048]{1,0:T(8,128)(2,1)} %q_hbm.1, bf16[128,2048]{1,0:T(8,128)(2,1)} %k_hbm.1, bf16[128,2048]{1,0:T(8,128)(2,1)} %v_hbm.1, f32[16,128]{1,0:T(8,128)} %ridge_ref.1), custom_call_target="tpu_custom_call" | custom-call | tf_op jit(solution)/shard_map/pallas_call | solution.py:381
  60.8 1.9 %copy.6 = bf16[128,2048]{1,0:T(8,128)(2,1)} copy(bf16[128,2048]{1,0:T(8,128)(2,1)} %shard_map.46) | data formatting | bytes 1048576

commit v5 on v4

--- a/solution.py
+++ b/solution.py
@@ -82,7 +82,7 @@
     return fresh
 
 
-def invert_all(sys_ref, pinv_ref):
+def invert_all(sys_ref, pinv_ref, after_first):
     count = sys_ref.shape[0]
     packs = count // PACK
     lane = lax.broadcasted_iota(jnp.int32, (8, DK), 1)
@@ -93,6 +93,10 @@
     lane128 = lax.broadcasted_iota(jnp.int32, (DK, DK), 1) // EDGE
 
     def panel(p, carry):
+        @pl.when(p == 1)
+        def _():
+            after_first()
+
         start = pl.multiple_of(p * EDGE, EDGE)
         all_rows = []
         for g in range(packs):
@@ -137,7 +141,7 @@
 
 def whole_kernel(
     owners, shards, q_hbm, k_hbm, v_hbm, ridge_ref, out_hbm,
-    q_all, k_all, v_all, sys_ref, vk_ref, pinv_ref, stage, gram_total, vk_total, gram_slots, vk_slots,
+    q_all, k_all, v_all, sys_ref, vk_ref, pinv_ref, stage, before, gram_total, vk_total, gram_slots, vk_slots,
     send_sems, recv_sems, local_sems, out_send, out_recv, out_local, gram_send, gram_recv, vk_send, vk_recv,
 ):
     me, shard = lax.axis_index("head"), lax.axis_index("seq")
@@ -190,7 +194,7 @@
         )
 
     def send_totals(total, slots, send, recv):
-        for far in reversed(range(1, shards)):
+        for far in range(1, shards):
             @pl.when(shard + far < shards)
             def _():
                 total_copy(total, slots, send, recv, far, shard + far).start()
@@ -271,7 +275,6 @@
     runs = lax.fori_loop(0, owners, values_in, zero)
     for h in range(heads):
         vk_total[h] = runs[h]
-    send_totals(vk_total, vk_slots, vk_send, vk_recv)
 
     def sum_slots(slots, total):
         for h in range(heads):
@@ -283,10 +286,9 @@
                     total[h] = total[h] + slots[far - 1, h]
 
     wait_totals(gram_total, gram_slots, gram_send, gram_recv)
-    drain_totals(gram_total, gram_slots, gram_send, gram_recv)
-    sum_slots(gram_slots, gram_total)
+    sum_slots(gram_slots, before)
     for h in range(heads):
-        extra = gram_total[h]
+        extra = before[h]
 
         def add(c, carry):
             sys_ref[h * groups + c] = sys_ref[h * groups + c] + extra
@@ -294,11 +296,10 @@
 
         lax.fori_loop(0, groups, add, 0)
 
-    invert_all(sys_ref, pinv_ref)
+    invert_all(sys_ref, pinv_ref, lambda: send_totals(vk_total, vk_slots, vk_send, vk_recv))
 
     wait_totals(vk_total, vk_slots, vk_send, vk_recv)
-    drain_totals(vk_total, vk_slots, vk_send, vk_recv)
-    sum_slots(vk_slots, vk_total)
+    sum_slots(vk_slots, before)
     for step in range(1, owners):
         incoming(2, lax.rem(me + step, owners)).wait_recv()
 
@@ -332,7 +333,7 @@
             ku = jnp.concatenate([ku, ku, ku], axis=1)
             scores.append(dot(jnp.concatenate([high, mid, low], axis=1), ku, (1, 1)))
             left = jnp.concatenate([high, high, mid, high, low, mid], axis=1)
-            start = vk_ref[h * groups + source * per_source + i] + vk_total[h]
+            start = vk_ref[h * groups + source * per_source + i] + before[h]
             carried.append(dot(left, right_stack(split3(start)), (1, 0)))
         for (h, i), score, carry_in in zip(jobs, scores, carried):
             score = jnp.where(causal, score, 0.0)
@@ -367,6 +368,8 @@
             device_id_type=pl.DeviceIdType.MESH,
         ).wait_recv()
     mine.wait()
+    drain_totals(gram_total, gram_slots, gram_send, gram_recv)
+    drain_totals(vk_total, vk_slots, vk_send, vk_recv)
 
 
 def body(queries, key_rows, value_rows, ridge_diag):
@@ -393,6 +396,7 @@
             pltpu.VMEM((owners, rows, width), BF16),
             pltpu.VMEM((heads, DK, DK), F32),
             pltpu.VMEM((heads, DK, DK), F32),
+            pltpu.VMEM((heads, DK, DK), F32),
             pltpu.VMEM((shards - 1, heads, DK, DK), F32),
             pltpu.VMEM((shards - 1, heads, DK, DK), F32),
             dma((3, owners)), dma((3, owners)), dma((3,)),

time: 62.9 us -> 61.2 us (0.973)
  the two profiles are of different devices: /device:TPU:19 before, /device:TPU:27 now
where the time goes in v5:
time: 61.2 us; the launch traced here: 61 us
  Pallas kernels  59.1 us (97%)
  local copies, waits for them, and re-layouts  1.88 us (3%)
    pallas_call x1, Pallas kernels, body(): pl.pallas_call(functools.partial(whole_kernel, owners, shards), out_shape...  59.1 us
    unnamed x1, local copies, waits for them, and re-layouts  1.88 us

profile of v5, /device:TPU:27, one launch (start us, length us, event | category | flops | bytes accessed | tf_op | source)
XLA Modules:
  0.0 61.0 jit_solution(8983692862300007177)
XLA Ops:
  0.0 59.1 %shard_map.46 = bf16[128,2048]{1,0:T(8,128)(2,1)} custom-call(bf16[128,2048]{1,0:T(8,128)(2,1)} %q_hbm.1, bf16[128,2048]{1,0:T(8,128)(2,1)} %k_hbm.1, bf16[128,2048]{1,0:T(8,128)(2,1)} %v_hbm.1, f32[16,128]{1,0:T(8,128)} %ridge_ref.1), custom_call_target="tpu_custom_call" | custom-call | tf_op jit(solution)/shard_map/pallas_call | solution.py:384
  59.1 1.9 %copy.6 = bf16[128,2048]{1,0:T(8,128)(2,1)} copy(bf16[128,2048]{1,0:T(8,128)(2,1)} %shard_map.46) | data formatting | bytes 1048576
